TPU v7x, 128 devices: a whole 4x4x4 slice. The times are simulated.
128 devices in a mesh: prow: 32 (over x, z_lo, y), pcol: 4 (over z_hi, core).
Axes of the slice: x: 4, y: 4, z: 4 (z_hi: 2, z_lo: 2; z = z_hi * 2 + z_lo), core: 2. Of those that a mesh axis runs over, the one named last changes fastest.
Arguments:
- inverse_band: float32 [4096, 4096], P('prow', 'pcol'), may hold values from -0.09375 to 0.09375
- factor_panel: float32 [2, 4096, 512], P(None, 'prow', 'pcol'), may hold values from -0.6 to 0.6
- diag_inverse: float32 [2, 512, 512], replicated, may hold values from -1 to 2, as said below
- ancestors: int32 [2, 63], replicated, may hold values from 0 to 63, as said below
- counts: int32 [2], replicated, may hold values from 1 to 63, as said below
Outputs:
- new_column: float32 [2, 4096, 512], P(None, 'prow', 'pcol')
- diag_block: float32 [2, 512, 512], P(None, 'prow', 'pcol')
Inputs may be any that keep to these rules, and one draw needn't show every extreme that they name: Each row holds distinct block numbers; its first counts[s] entries are in increasing order and include 63; the entries after them are other block numbers, which are not ancestors. One of the two counts is 63; the other is below 63. `diag_inverse`: lower triangular; diagonal entries from 0.5 to 2.
All inputs are finite; a program needn't handle non-finite values.
Results may differ from a plain program's by a relative error of at most 0.000073.
Values sent between devices are 32-bit elements; how exact they have to be, the bound alone decides.
No kernel may reach another device: no remote copies, remote signals or barrier semaphores. Data moves between devices by JAX's collectives and lax.ppermute only.
A program may use at most 64 MiB of HBM per device.

v0:
```python
import jax
import jax.numpy as jnp
from jax import lax
from jax.sharding import PartitionSpec as P

W = 512
BS = 64
precise = lax.Precision.HIGHEST


def local(inverse_band, factor_panel, diag_inverse, ancestors, counts):
    row_index = lax.axis_index("prow")
    col_index = lax.axis_index("pcol")
    row_devices = lax.axis_size("prow")
    col_devices = lax.axis_size("pcol")
    supernodes = factor_panel.shape[0]
    band_rows = factor_panel.shape[1]
    blocks = band_rows // BS
    quarter = W // col_devices
    block_ids = jnp.arange(blocks, dtype=jnp.int32) * row_devices + row_index
    filled = jnp.arange(ancestors.shape[1], dtype=jnp.int32)[None, :] < counts[:, None]
    matches = (ancestors[:, :, None] == block_ids[None, None, :]) & filled[:, :, None]
    members = jnp.any(matches, axis=1).astype(jnp.float32)
    row_mask = jnp.repeat(members, BS, axis=1)[:, :, None]
    full_panel = lax.all_gather(factor_panel, "pcol", axis=2, tiled=True)
    scaled_panel = (
        jnp.einsum("srk,skw->srw", full_panel, diag_inverse, precision=precise) * row_mask
    )
    own_part = lax.dynamic_slice_in_dim(scaled_panel, col_index * quarter, quarter, 2)
    collected = lax.all_gather(own_part, "prow", axis=1, tiled=True)
    grouped = collected.reshape(
        supernodes, row_devices // col_devices, col_devices, band_rows, quarter
    )
    incoming = lax.all_to_all(grouped, "pcol", split_axis=2, concat_axis=4, tiled=True)
    stacked = incoming.reshape(incoming.shape[0], -1, incoming.shape[-1])
    partial_sums = jnp.einsum("rc,scw->srw", inverse_band, stacked, precision=precise)
    summed = lax.psum_scatter(partial_sums, "pcol", scatter_dimension=2, tiled=True)
    applied = summed * row_mask
    new_column = -applied
    diag_rows = W // row_devices
    product = jnp.einsum("src,srw->csw", scaled_panel, applied, precision=precise)
    reduced = lax.psum_scatter(
        product.reshape(lax.axis_size("prow") * diag_rows, -1),
        "prow",
        scatter_dimension=0,
        tiled=True,
    )
    reduced = reduced.reshape(diag_rows, supernodes, quarter).transpose(1, 0, 2)
    row_factor = lax.dynamic_slice_in_dim(diag_inverse, row_index * diag_rows, diag_rows, 2)
    col_factor = lax.dynamic_slice_in_dim(diag_inverse, col_index * quarter, quarter, 2)
    diag_block = jnp.einsum("skr,skw->srw", row_factor, col_factor, precision=precise) + reduced
    return (new_column, diag_block)


def solution(mesh):
    in_specs = (P("prow", "pcol"), P(None, "prow", "pcol"), P(), P(), P())
    out_specs = (P(None, "prow", "pcol"), P(None, "prow", "pcol"))
    return jax.shard_map(local, mesh=mesh, in_specs=in_specs, out_specs=out_specs, check_vma=False)
```

profile of v0, /device:TPU:0, one launch (start us, length us, event | category | flops | bytes accessed | tf_op | source)
XLA Modules:
  0.0 451.2 jit_solution(8875050085147239257)
XLA Ops:
  7.2 0.0 copy-start
  7.2 0.0 all-gather.2.cloned.1.call-start
  7.2 0.9 iota_compare_fusion
  8.1 0.9 and_reduce_fusion
  9.0 0.1 broadcast_in_dim.2
  9.1 0.1 mul.33
  9.1 9.9 %all_gather.6 = f32[2,128,512]{2,1,0:T(8,128)S(1)} all-gather(f32[2,128,128]{2,1,0:T(8,128)} %param.6), channel_id=1, replica_groups=mesh['prow'=32,'pcol'=4] {'pcol'}, dimensions={2}, use_global_device_ids=true | all-gather | bytes 655360 | tf_op jit(solution)/shard_map/all_gather | solution.py:25
  19.0 0.0 copy-done
  19.0 1.3 convolution_multiply_fusion
  20.3 0.7 constant_dynamic-slice_fusion
  21.0 0.0 all-gather.2.cloned.1.call-update
  21.0 0.0 reduce-scatter.3.cloned.1.call-start
  21.1 157.6 %all-gather.2.cloned.1.call-done = f32[2,4096,128]{2,1,0:T(8,128)} async-done(((f32[2,128,128]{2,1,0:T(8,128)}), f32[2,4096,128]{2,1,0:T(8,128)}) %all-gather.2.cloned.1.call-update) | async-done | bytes 4194320 | tf_op jit(solution)/shard_map/all_gather | solution.py:30
  178.7 2.5 copy.21
  181.1 53.7 %all_to_all.15 = f32[2,8,4,128,128]{4,3,1,0,2:T(8,128)} all-to-all(f32[2,8,4,128,128]{4,3,1,0,2:T(8,128)S(1)} %copy.21), channel_id=1, replica_groups=mesh['prow'=32,'pcol'=4] {'pcol'}, dimensions={2} | all-to-all | bytes 8388608 | tf_op jit(solution)/shard_map/all_to_all | solution.py:34
  234.9 5.2 %copy.22 = f32[2,8,1,128,4,128]{3,1,5,4,0,2:T(8,128)} copy(f32[2,8,1,128,4,128]{5,3,1,0,4,2:T(8,128)} %bitcast.31) | data formatting | bytes 8388608 | tf_op jit(solution)/shard_map/all_to_all | solution.py:34
  240.1 0.0 copy-start.1
  240.1 5.0 %reshape.46 = f32[2,1024,512]{1,2,0:T(8,128)} reshape(f32[2,8,1,128,4,128]{3,1,5,4,0,2:T(8,128)} %copy.22) | data formatting | bytes 8388608 | tf_op jit(solution)/shard_map/reshape | solution.py:35
  245.1 0.0 copy-done.1
  245.1 6.4 %convolution_bitcast_fusion = f32[2,128,512]{1,2,0:T(8,128)} fusion(f32[2,1024,512]{1,2,0:T(8,128)} %reshape.46, f32[128,1024]{1,0:T(8,128)S(1)} %copy-done.1), kind=kOutput, calls=%fused_computation | convolution fusion | flops 1610612736 | bytes 5242880 | tf_op jit(solution)/shard_map/rc,scw->srw/dot_general | solution.py:36
  251.5 0.0 reduce-scatter.3.cloned.1.call-update
  251.5 0.0 reduce-scatter.5.cloned.1.call-start
  251.6 27.0 %reduce-scatter.3.cloned.1.call-done = f32[2,128,128]{1,2,0:T(8,128)} async-done(((f32[2,128,512]{1,2,0:T(8,128)}), f32[2,128,128]{1,2,0:T(8,128)}) %reduce-scatter.3.cloned.1.call-update) | async-done | bytes 131088 | tf_op jit(solution)/shard_map/reduce_scatter | solution.py:37
  278.5 1.5 fusion.3
  280.0 1.0 copy.24
  281.0 0.0 reduce-scatter.5.cloned.1.call-update
  281.0 0.9 multiply_negate_fusion
  282.0 0.8 copy.26
  282.7 159.5 %reduce-scatter.5.cloned.1.call-done = f32[16,256]{1,0:T(8,128)} async-done(((f32[512,256]{1,0:T(8,128)}), f32[16,256]{1,0:T(8,128)}) %reduce-scatter.5.cloned.1.call-update) | async-done | bytes 16400 | tf_op jit(solution)/shard_map/reduce_scatter | solution.py:42
  442.2 2.5 convolution_add_fusion
  (2 shorter events, 0.0 us)
Async XLA Ops:
  7.2 11.8 %copy-start = (f32[2,512,512]{2,1,0:T(8,128)S(1)}, f32[2,512,512]{2,1,0:T(8,128)}, u32[]{:S(2)}) copy-start(f32[2,512,512]{2,1,0:T(8,128)} %param.7) | copy-start | bytes 6291460
  7.2 171.5 %all-gather.2.cloned.1.call-start = ((), (), s32[]{:S(2)}) async-start(), calls=%async_computation.3 | async-start | bytes 4325376 | tf_op jit(solution)/shard_map/all_gather | solution.py:30
  21.0 257.5 %reduce-scatter.3.cloned.1.call-start = ((), (), s32[]{:S(2)}) async-start(), calls=%async_computation.4 | async-start | bytes 655360 | tf_op jit(solution)/shard_map/reduce_scatter | solution.py:37
  240.1 5.0 %copy-start.1 = (f32[128,1024]{1,0:T(8,128)S(1)}, f32[128,1024]{1,0:T(8,128)}, u32[]{:S(2)}) copy-start(f32[128,1024]{1,0:T(8,128)} %param.5) | copy-start | bytes 1572868
  251.5 190.7 %reduce-scatter.5.cloned.1.call-start = ((), (), s32[]{:S(2)}) async-start(), calls=%async_computation.5 | async-start | bytes 540672 | tf_op jit(solution)/shard_map/reduce_scatter | solution.py:42
Sparse Core Ops, SparseCore 0:
  21.1 157.5 all-gather.1
  251.6 26.8 reduce-scatter.2
  281.2 161.0 reduce-scatter.4
where the time goes:
time: 452 us; the launch traced here: 451 us
  waiting for transfers between devices  344 us (76%)
  blocking collectives  63.6 us (14%)
  local copies, waits for them, and re-layouts  15.3 us (3%)
  between operations  13.8 us (3%)
  matrix products  11.7 us (3%)
    reduce_scatter x1, waiting for transfers between devices, local(): lax.psum_scatter(product.reshape(lax.axis_size('prow') * diag_rows, -1),...  159 us
    all_gather x1, waiting for transfers between devices, local(): collected = lax.all_gather(own_part, 'prow', axis=1, tiled=True)  158 us
    all_to_all x1, blocking collectives, local(): lax.all_to_all(grouped, 'pcol', split_axis=2, concat_axis=4, tiled=True)  53.7 us
    reduce_scatter x1, waiting for transfers between devices, local(): lax.psum_scatter(partial_sums, 'pcol', scatter_dimension=2, tiled=True)  27 us
    all_gather x1, blocking collectives, local(): full_panel = lax.all_gather(factor_panel, 'pcol', axis=2, tiled=True)  9.87 us
  transfers between devices with their start and end apart: 3, of which 3 were waited for; matrix products, arithmetic and copies ran while one was open for 0% of the time, Pallas kernels for 0%

commit v1 on v0

--- a/solution.py
+++ b/solution.py
@@ -27,7 +27,7 @@
         jnp.einsum("srk,skw->srw", full_panel, diag_inverse, precision=precise) * row_mask
     )
     own_part = lax.dynamic_slice_in_dim(scaled_panel, col_index * quarter, quarter, 2)
-    collected = lax.all_gather(own_part, "prow", axis=1, tiled=True)
+    collected = jnp.concatenate(lax.all_gather(own_part, "prow"), axis=1)
     grouped = collected.reshape(
         supernodes, row_devices // col_devices, col_devices, band_rows, quarter
     )

time: 452 us -> 452 us (level)
    another operation x0 -> x1, local copies, waits for them, and re-layouts: none -> 5.25 us  [local(): collected.reshape(supernodes, row_devices // col_devices, col_devices, ba...]
where the time goes in v1:
time: 452 us; the launch traced here: 451 us
  waiting for transfers between devices  344 us (76%)
  blocking collectives  63.7 us (14%)
  local copies, waits for them, and re-layouts  15 us (3%)
  between operations  13.8 us (3%)
  matrix products  11.6 us (3%)
    reduce_scatter x1, waiting for transfers between devices, local(): lax.psum_scatter(product.reshape(lax.axis_size('prow') * diag_rows, -1),...  159 us
    all_gather x1, waiting for transfers between devices, local(): collected = jnp.concatenate(lax.all_gather(own_part, 'prow'), axis=1)  158 us
    all_to_all x1, blocking collectives, local(): lax.all_to_all(grouped, 'pcol', split_axis=2, concat_axis=4, tiled=True)  53.8 us
    reduce_scatter x1, waiting for transfers between devices, local(): lax.psum_scatter(partial_sums, 'pcol', scatter_dimension=2, tiled=True)  27.1 us
    all_gather x1, blocking collectives, local(): full_panel = lax.all_gather(factor_panel, 'pcol', axis=2, tiled=True)  9.87 us
  transfers between devices with their start and end apart: 3, of which 3 were waited for; matrix products, arithmetic and copies ran while one was open for 0% of the time, Pallas kernels for 0%

profile of v1, /device:TPU:0, one launch (start us, length us, event | category | flops | bytes accessed | tf_op | source)
XLA Modules:
  0.0 451.2 jit_solution(14815678304134145412)
XLA Ops:
  7.2 0.0 copy-start
  7.2 0.0 all-gather.3.cloned.1.call-start
  7.2 0.9 iota_compare_fusion
  8.1 0.9 and_reduce_fusion
  9.0 0.1 broadcast_in_dim.2
  9.1 0.1 mul.33
  9.1 9.9 %all_gather.9 = f32[2,128,512]{2,1,0:T(8,128)S(1)} all-gather(f32[2,128,128]{2,1,0:T(8,128)} %param.6), channel_id=1, replica_groups=mesh['prow'=32,'pcol'=4] {'pcol'}, dimensions={2}, use_global_device_ids=true | all-gather | bytes 655360 | tf_op jit(solution)/shard_map/all_gather | solution.py:25
  19.0 0.0 copy-done
  19.0 1.3 convolution_multiply_fusion
  20.3 0.7 constant_dynamic-slice_fusion
  21.0 0.0 all-gather.3.cloned.1.call-update
  21.0 0.0 reduce-scatter.3.cloned.1.call-start
  21.1 157.5 %all-gather.3.cloned.1.call-done = f32[64,128,128]{2,1,0:T(8,128)} async-done(((f32[2,128,128]{2,1,0:T(8,128)}), f32[64,128,128]{2,1,0:T(8,128)}) %all-gather.3.cloned.1.call-update) | async-done | bytes 4194320 | tf_op jit(solution)/shard_map/all_gather | solution.py:30
  178.6 5.2 %copy.34 = f32[2,8,4,128,128]{3,1,4,0,2:T(8,128)} copy(f32[2,8,4,128,128]{4,3,0,2,1:T(8,128)} %bitcast.36) | data formatting | bytes 8388608 | tf_op jit(solution)/shard_map/reshape;reshape | solution.py:31
  183.8 53.8 %all_to_all.15 = f32[2,8,4,128,128]{3,1,4,0,2:T(8,128)S(1)} all-to-all(f32[2,8,4,128,128]{3,1,4,0,2:T(8,128)} %copy.34), channel_id=1, replica_groups=mesh['prow'=32,'pcol'=4] {'pcol'}, dimensions={2} | all-to-all | bytes 8388608 | tf_op jit(solution)/shard_map/all_to_all | solution.py:34
  237.7 2.3 copy.35
  239.9 0.0 copy-start.1
  239.9 4.9 %reshape.46 = f32[2,1024,512]{1,2,0:T(8,128)} reshape(f32[2,8,1,128,4,128]{3,1,5,4,0,2:T(8,128)} %copy.35) | data formatting | bytes 8388608 | tf_op jit(solution)/shard_map/reshape | solution.py:35
  244.9 0.0 copy-done.1
  244.9 6.4 %convolution_bitcast_fusion = f32[2,128,512]{1,2,0:T(8,128)} fusion(f32[2,1024,512]{1,2,0:T(8,128)} %reshape.46, f32[128,1024]{1,0:T(8,128)S(1)} %copy-done.1), kind=kOutput, calls=%fused_computation | convolution fusion | flops 1610612736 | bytes 5242880 | tf_op jit(solution)/shard_map/rc,scw->srw/dot_general | solution.py:36
  251.3 0.0 reduce-scatter.3.cloned.1.call-update
  251.3 0.0 reduce-scatter.5.cloned.1.call-start
  251.3 27.1 %reduce-scatter.3.cloned.1.call-done = f32[2,128,128]{1,2,0:T(8,128)} async-done(((f32[2,128,512]{1,2,0:T(8,128)}), f32[2,128,128]{1,2,0:T(8,128)}) %reduce-scatter.3.cloned.1.call-update) | async-done | bytes 131088 | tf_op jit(solution)/shard_map/reduce_scatter | solution.py:37
  278.5 1.5 fusion.3
  280.0 1.0 copy.37
  281.0 0.0 reduce-scatter.5.cloned.1.call-update
  281.0 0.9 multiply_negate_fusion
  281.9 0.8 copy.39
  282.7 159.5 %reduce-scatter.5.cloned.1.call-done = f32[16,256]{1,0:T(8,128)} async-done(((f32[512,256]{1,0:T(8,128)}), f32[16,256]{1,0:T(8,128)}) %reduce-scatter.5.cloned.1.call-update) | async-done | bytes 16400 | tf_op jit(solution)/shard_map/reduce_scatter | solution.py:42
  442.1 2.5 convolution_add_fusion
  (2 shorter events, 0.0 us)
Async XLA Ops:
  7.2 11.8 %copy-start = (f32[2,512,512]{2,1,0:T(8,128)S(1)}, f32[2,512,512]{2,1,0:T(8,128)}, u32[]{:S(2)}) copy-start(f32[2,512,512]{2,1,0:T(8,128)} %param.7) | copy-start | bytes 6291460
  7.2 171.4 %all-gather.3.cloned.1.call-start = ((), (), s32[]{:S(2)}) async-start(), calls=%async_computation.5 | async-start | bytes 4325376 | tf_op jit(solution)/shard_map/all_gather | solution.py:30
  21.0 257.5 %reduce-scatter.3.cloned.1.call-start = ((), (), s32[]{:S(2)}) async-start(), calls=%async_computation.3 | async-start | bytes 655360 | tf_op jit(solution)/shard_map/reduce_scatter | solution.py:37
  239.9 4.9 %copy-start.1 = (f32[128,1024]{1,0:T(8,128)S(1)}, f32[128,1024]{1,0:T(8,128)}, u32[]{:S(2)}) copy-start(f32[128,1024]{1,0:T(8,128)} %param.5) | copy-start | bytes 1572868
  251.3 190.9 %reduce-scatter.5.cloned.1.call-start = ((), (), s32[]{:S(2)}) async-start(), calls=%async_computation.4 | async-start | bytes 540672 | tf_op jit(solution)/shard_map/reduce_scatter | solution.py:42
Sparse Core Ops, SparseCore 0:
  21.1 157.4 all-gather.2
  251.4 27.0 reduce-scatter.2
  281.1 161.0 reduce-scatter.4
